TPU v7x, 32 devices: a whole 2x2x4 slice. The times are simulated.
32 devices in a mesh: rep: 8 (over z, core), shard: 4 (over y, x).
Axes of the slice: x: 2, y: 2, z: 4, core: 2. Of those that a mesh axis runs over, the one named last changes fastest.
Arguments:
- tokens: bfloat16 [4096, 1536], P(('rep', 'shard')), may hold values from -6 to 6
- cotangent: bfloat16 [4096, 1536], P(('rep', 'shard')), may hold values from -6 to 6
- lengths: int32 [8], P('rep'), may hold values from 128 to 512, as said below
- gain_one: bfloat16 [1536], P('shard'), may hold values from 0.5 to 1.5
- w_query: bfloat16 [1536, 1536], P('shard'), may hold values from -0.15625 to 0.15625
- w_key: bfloat16 [1536, 1536], P('shard'), may hold values from -0.15625 to 0.15625
- w_value: bfloat16 [1536, 1536], P('shard'), may hold values from -0.15625 to 0.15625
- w_path: bfloat16 [1536, 1536], P('shard'), may hold values from -0.15625 to 0.15625
- w_beta: bfloat16 [1536, 12], P('shard'), may hold values from -0.15625 to 0.15625
- w_out: bfloat16 [1536, 1536], P('shard'), may hold values from -0.625 to 0.625
- gain_two: bfloat16 [1536], P('shard'), may hold values from 0.5 to 1.5
- w_gate: bfloat16 [1536, 4096], P('shard'), may hold values from -0.15625 to 0.15625
- w_up: bfloat16 [1536, 4096], P('shard'), may hold values from -0.15625 to 0.15625
- w_down: bfloat16 [4096, 1536], P('shard'), may hold values from -0.09375 to 0.09375
Outputs:
- output: bfloat16 [4096, 1536], P(('rep', 'shard'))
- input_grad: bfloat16 [4096, 1536], P(('rep', 'shard'))
- grad_gain_one: float32 [1536], P('shard')
- grad_w_query: float32 [1536, 1536], P('shard')
- grad_w_key: float32 [1536, 1536], P('shard')
- grad_w_value: float32 [1536, 1536], P('shard')
- grad_w_path: float32 [1536, 1536], P('shard')
- grad_w_beta: float32 [1536, 12], P('shard')
- grad_w_out: float32 [1536, 1536], P('shard')
- grad_gain_two: float32 [1536], P('shard')
- grad_w_gate: float32 [1536, 4096], P('shard')
- grad_w_up: float32 [1536, 4096], P('shard')
- grad_w_down: float32 [4096, 1536], P('shard')
- rms_input: float32 [], replicated
- rms_attn: float32 [], replicated
- rms_feed: float32 [], replicated
Inputs may be any that keep to these rules, and one draw needn't show every extreme that they name: Sequence r fills the first lengths[r] of its 512 slots; at least one sequence fills all of them.
All inputs are finite; a program needn't handle non-finite values.
Results may differ from a plain program's by a relative error of at most 0.02.
Values may be sent and summed in bfloat16 or wider, within the bound.
No kernel may reach another device: no remote copies, remote signals or barrier semaphores. Data moves between devices by JAX's collectives and lax.ppermute only.
A program may use at most 320 MiB of HBM per device.

v0:
```python
import jax
import jax.numpy as jnp
from jax import lax
from jax.sharding import PartitionSpec as P

eps = 1e-06
highest = lax.Precision.HIGHEST


def rms_norm(value, gain_vec):
    factor = lax.rsqrt(jnp.mean(value * value, axis=-1, keepdims=True) + eps)
    return value * factor * gain_vec


def unit_rows(raw):
    return raw * lax.rsqrt(jnp.sum(raw * raw, axis=-1, keepdims=True) + eps)


def rounded(value):
    return lax.optimization_barrier(value.astype(jnp.bfloat16)).astype(jnp.float32)


def round_pass(value):
    return value + lax.stop_gradient(rounded(value) - value)


def split_heads(matrix, head_count):
    return matrix.reshape(matrix.shape[0], head_count, -1).transpose(1, 0, 2)


def join_heads(matrix):
    return matrix.transpose(1, 0, 2).reshape(matrix.shape[1], -1)


def mul_low(left, right):
    return jnp.dot(left, right, preferred_element_type=jnp.float32)


def back_mul(grad_rows, weight):
    return jnp.einsum("tg,fg->tf", grad_rows, weight, preferred_element_type=jnp.float32)


def weight_grad(left, right):
    return jnp.einsum("tf,tg->fg", left, right, preferred_element_type=jnp.float32)


def masks(block_len):
    row_ids = jnp.arange(block_len)[:, None]
    col_ids = jnp.arange(block_len)[None, :]
    return (col_ids < row_ids, col_ids <= row_ids)


def block_system(direction, beta_rate):
    block_len = direction.shape[1]
    strictly, up_to = masks(block_len)
    gram = jnp.einsum("htd,hsd->hts", direction, direction, precision=highest)
    return jnp.eye(block_len, dtype=jnp.float32)[None] + jnp.where(
        strictly[None], gram * beta_rate[:, None, :], 0.0
    )


def own_context(keyset, values, direction, beta_rate):
    system = block_system(direction, beta_rate)
    strictly, up_to = masks(keyset.shape[1])
    coupled = jnp.where(
        strictly[None], jnp.einsum("htd,hjd->htj", direction, keyset, precision=highest), 0.0
    )
    solved = jax.scipy.linalg.solve_triangular(system, coupled, lower=True, unit_diagonal=True)
    scaled_dir = direction * beta_rate[:, :, None]
    key_end = keyset - jnp.einsum("htj,htd->hjd", solved, scaled_dir, precision=highest)
    through = jax.scipy.linalg.solve_triangular(system, direction, lower=True, unit_diagonal=True)
    block_map = jnp.eye(direction.shape[2], dtype=jnp.float32)[None] - jnp.einsum(
        "htm,htn->hmn", scaled_dir, through, precision=highest
    )
    return (join_heads(key_end), join_heads(values), block_map[None])


def attend(
    queries, keyset, values, direction, beta_rate, key_far, value_far, maps_far, my_block, length
):
    head_count, block_len, head_width = queries.shape
    blocks = maps_far.shape[0]
    score_scale = head_width ** (-0.5)
    strictly, up_to = masks(block_len)
    system = block_system(direction, beta_rate)
    coupled = jnp.where(
        strictly[None], jnp.einsum("htd,hjd->htj", direction, keyset, precision=highest), 0.0
    )
    solved = jax.scipy.linalg.solve_triangular(system, coupled, lower=True, unit_diagonal=True)
    crossing = (
        jnp.where(
            up_to[None], jnp.einsum("hid,htd->hit", queries, direction, precision=highest), 0.0
        )
        * beta_rate[:, None, :]
    )
    near_scores = (
        jnp.einsum("hid,hjd->hij", queries, keyset, precision=highest)
        - jnp.einsum("hit,htj->hij", crossing, solved, precision=highest)
    ) * score_scale
    back_solved = jax.scipy.linalg.solve_triangular(
        system, crossing.transpose(0, 2, 1), lower=True, trans=1, unit_diagonal=True
    )
    moved = queries - jnp.einsum("hti,htd->hid", back_solved, direction, precision=highest)

    def advance(carried, item_pair):
        block_map, index = item_pair
        updated = jnp.einsum("hid,hde->hie", carried, block_map, precision=highest)
        return (jnp.where(index < my_block, updated, carried), carried)

    unused, reached = lax.scan(advance, moved, (maps_far, jnp.arange(blocks)), reverse=True)
    far_keys = key_far.reshape(blocks, block_len, head_count, head_width)
    far_values = value_far.reshape(blocks, block_len, head_count, head_width)
    far_scores = jnp.einsum("ehid,ejhd->ehij", reached, far_keys, precision=highest) * score_scale
    positions = jnp.arange(block_len)
    near_ok = up_to[None] & ((my_block * block_len + positions)[None, None, :] < length)
    block_ids = jnp.arange(blocks)
    far_ok = (block_ids[:, None, None, None] < my_block) & (
        (block_ids[:, None] * block_len + positions[None, :])[:, None, None, :] < length
    )
    near_masked = jnp.where(near_ok, near_scores, -1e30)
    far_masked = jnp.where(far_ok, far_scores, -1e30)
    row_max = jnp.maximum(jnp.max(near_masked, axis=2), jnp.max(far_masked, axis=(0, 3)))[
        :, :, None
    ]
    row_total = jnp.sum(jnp.where(near_ok, jnp.exp(near_masked - row_max), 0.0), axis=2) + jnp.sum(
        jnp.where(far_ok, jnp.exp(far_masked - row_max[None]), 0.0), axis=(0, 3)
    )
    log_total = row_max + jnp.log(row_total)[:, :, None]
    near_probs = round_pass(jnp.where(near_ok, jnp.exp(near_masked - log_total), 0.0))
    far_probs = round_pass(jnp.where(far_ok, jnp.exp(far_masked - log_total[None]), 0.0))
    return jnp.einsum("hij,hjd->hid", near_probs, values, precision=highest) + jnp.einsum(
        "ehij,ejhd->hid", far_probs, far_values, precision=highest
    )


def per_device(
    tokens,
    cotangent,
    lengths,
    gain_one,
    w_query,
    w_key,
    w_value,
    w_path,
    w_beta,
    w_out,
    gain_two,
    w_gate,
    w_up,
    w_down,
):
    gain_a, query_w, key_w, value_w, path_w, beta_w, out_w, gain_b, gate_w, up_w, down_w = (
        lax.all_gather(gain_one, "shard", axis=0, tiled=True),
        lax.all_gather(w_query, "shard", axis=0, tiled=True),
        lax.all_gather(w_key, "shard", axis=0, tiled=True),
        lax.all_gather(w_value, "shard", axis=0, tiled=True),
        lax.all_gather(w_path, "shard", axis=0, tiled=True),
        lax.all_gather(w_beta, "shard", axis=0, tiled=True),
        lax.all_gather(w_out, "shard", axis=0, tiled=True),
        lax.all_gather(gain_two, "shard", axis=0, tiled=True),
        lax.all_gather(w_gate, "shard", axis=0, tiled=True),
        lax.all_gather(w_up, "shard", axis=0, tiled=True),
        lax.all_gather(w_down, "shard", axis=0, tiled=True),
    )
    block_len = tokens.shape[0]
    width = tokens.shape[1]
    head_count = beta_w.shape[1]
    my_block = lax.axis_index("shard")
    length = lengths[0]
    live_mask = (my_block * block_len + jnp.arange(block_len) < length).astype(jnp.float32)[:, None]
    stream_in = tokens.astype(jnp.float32)
    normed_f, norm_pull = jax.vjp(rms_norm, stream_in, gain_a.astype(jnp.float32))
    normed = normed_f.astype(jnp.bfloat16)
    queries = split_heads(rounded(mul_low(normed, query_w)), head_count)
    keyset = split_heads(rounded(mul_low(normed, key_w)), head_count)
    values_h = split_heads(rounded(mul_low(normed, value_w)), head_count)
    raw = mul_low(normed, path_w).reshape(block_len, head_count, -1)
    direction_f, unit_pull = jax.vjp(unit_rows, raw)
    direction = rounded(direction_f).transpose(1, 0, 2)
    beta_rate = 2.0 * jax.nn.sigmoid(mul_low(normed, beta_w))
    (key_end, value_own, map_own), context_pull = jax.vjp(
        own_context, keyset, values_h, direction, beta_rate.T
    )
    key_far, value_far, maps_far = (
        lax.all_gather(key_end.astype(jnp.bfloat16), "shard", axis=0, tiled=True).astype(
            key_end.dtype
        ),
        lax.all_gather(value_own.astype(jnp.bfloat16), "shard", axis=0, tiled=True).astype(
            value_own.dtype
        ),
        lax.all_gather(map_own.astype(jnp.bfloat16), "shard", axis=0, tiled=True).astype(
            map_own.dtype
        ),
    )

    def local_attend(
        queries, keyset, values_h, direction, beta_heads, key_far, value_far, maps_far
    ):
        return attend(
            queries,
            keyset,
            values_h,
            direction,
            beta_heads,
            key_far,
            value_far,
            maps_far,
            my_block,
            length,
        )

    heads_out, attend_pull = jax.vjp(
        local_attend,
        queries,
        keyset,
        values_h,
        direction,
        beta_rate.T,
        key_far,
        value_far,
        maps_far,
    )
    mixed = join_heads(heads_out).astype(jnp.bfloat16)
    attn_out = mul_low(mixed, out_w)
    stream = stream_in + live_mask * attn_out
    normed_two_f, norm_two_pull = jax.vjp(rms_norm, stream, gain_b.astype(jnp.float32))
    normed_two = normed_two_f.astype(jnp.bfloat16)
    gate_pre = mul_low(normed_two, gate_w)
    up_pre = mul_low(normed_two, up_w)
    gate_sig = jax.nn.sigmoid(gate_pre)
    hidden = (gate_pre * gate_sig * up_pre).astype(jnp.bfloat16)
    feed_out = mul_low(hidden, down_w)
    output = (live_mask * (stream + feed_out)).astype(jnp.bfloat16)
    cot_rows = cotangent.astype(jnp.float32) * live_mask
    d_feed = cot_rows.astype(jnp.bfloat16)
    d_hidden = back_mul(d_feed, down_w)
    d_gate = (d_hidden * up_pre * gate_sig * (1.0 + gate_pre * (1.0 - gate_sig))).astype(
        jnp.bfloat16
    )
    d_up = (d_hidden * gate_pre * gate_sig).astype(jnp.bfloat16)
    d_normed_two = back_mul(d_gate, gate_w) + back_mul(d_up, up_w)
    d_stream_norm, grad_gain_b = norm_two_pull(d_normed_two)
    d_stream = cot_rows + d_stream_norm
    d_attn = (live_mask * d_stream).astype(jnp.bfloat16)
    d_mixed = split_heads(rounded(back_mul(d_attn, out_w)), head_count)
    (
        d_queries,
        d_keys_near,
        d_values_near,
        d_dir_near,
        d_beta_near,
        d_key_far,
        d_value_far,
        d_maps_far,
    ) = attend_pull(d_mixed)
    d_key_end, d_value_own, d_map_own = (
        lax.psum_scatter(
            d_key_far.astype(jnp.bfloat16), "shard", scatter_dimension=0, tiled=True
        ).astype(jnp.float32),
        lax.psum_scatter(
            d_value_far.astype(jnp.bfloat16), "shard", scatter_dimension=0, tiled=True
        ).astype(jnp.float32),
        lax.psum_scatter(
            d_maps_far.astype(jnp.bfloat16), "shard", scatter_dimension=0, tiled=True
        ).astype(jnp.float32),
    )
    d_keys_ctx, d_values_ctx, d_dir_ctx, d_beta_ctx = context_pull(
        (d_key_end, d_value_own, d_map_own)
    )
    d_query_b = join_heads(d_queries).astype(jnp.bfloat16)
    d_key_b = join_heads(d_keys_near + d_keys_ctx).astype(jnp.bfloat16)
    d_value_b = join_heads(d_values_near + d_values_ctx).astype(jnp.bfloat16)
    (d_raw,) = unit_pull((d_dir_near + d_dir_ctx).transpose(1, 0, 2))
    d_raw_b = d_raw.reshape(block_len, -1).astype(jnp.bfloat16)
    d_beta_total = (d_beta_near + d_beta_ctx).T
    d_logit_b = (d_beta_total * beta_rate * (1.0 - 0.5 * beta_rate)).astype(jnp.bfloat16)
    d_normed = (
        back_mul(d_query_b, query_w)
        + back_mul(d_key_b, key_w)
        + back_mul(d_value_b, value_w)
        + back_mul(d_raw_b, path_w)
        + back_mul(d_logit_b, beta_w)
    )
    d_stream_in, grad_gain_a = norm_pull(d_normed)
    input_grad = (d_stream_in + d_stream).astype(jnp.bfloat16)
    g_query = weight_grad(normed, d_query_b)
    g_key = weight_grad(normed, d_key_b)
    g_value = weight_grad(normed, d_value_b)
    g_path = weight_grad(normed, d_raw_b)
    g_beta = weight_grad(normed, d_logit_b)
    g_out = weight_grad(mixed, d_attn)
    g_gate = weight_grad(normed_two, d_gate)
    g_up = weight_grad(normed_two, d_up)
    g_down = weight_grad(hidden, d_feed)
    part_sums = (
        lax.psum_scatter(
            grad_gain_a.astype(jnp.bfloat16), "shard", scatter_dimension=0, tiled=True
        ).astype(jnp.float32),
        lax.psum_scatter(
            g_query.astype(jnp.bfloat16), "shard", scatter_dimension=0, tiled=True
        ).astype(jnp.float32),
        lax.psum_scatter(
            g_key.astype(jnp.bfloat16), "shard", scatter_dimension=0, tiled=True
        ).astype(jnp.float32),
        lax.psum_scatter(
            g_value.astype(jnp.bfloat16), "shard", scatter_dimension=0, tiled=True
        ).astype(jnp.float32),
        lax.psum_scatter(
            g_path.astype(jnp.bfloat16), "shard", scatter_dimension=0, tiled=True
        ).astype(jnp.float32),
        lax.psum_scatter(
            g_beta.astype(jnp.bfloat16), "shard", scatter_dimension=0, tiled=True
        ).astype(jnp.float32),
        lax.psum_scatter(
            g_out.astype(jnp.bfloat16), "shard", scatter_dimension=0, tiled=True
        ).astype(jnp.float32),
        lax.psum_scatter(
            grad_gain_b.astype(jnp.bfloat16), "shard", scatter_dimension=0, tiled=True
        ).astype(jnp.float32),
        lax.psum_scatter(
            g_gate.astype(jnp.bfloat16), "shard", scatter_dimension=0, tiled=True
        ).astype(jnp.float32),
        lax.psum_scatter(
            g_up.astype(jnp.bfloat16), "shard", scatter_dimension=0, tiled=True
        ).astype(jnp.float32),
        lax.psum_scatter(
            g_down.astype(jnp.bfloat16), "shard", scatter_dimension=0, tiled=True
        ).astype(jnp.float32),
    )
    owned = (
        lax.psum(part_sums[0].astype(jnp.bfloat16), "rep").astype(jnp.float32),
        lax.psum(part_sums[1].astype(jnp.bfloat16), "rep").astype(jnp.float32),
        lax.psum(part_sums[2].astype(jnp.bfloat16), "rep").astype(jnp.float32),
        lax.psum(part_sums[3].astype(jnp.bfloat16), "rep").astype(jnp.float32),
        lax.psum(part_sums[4].astype(jnp.bfloat16), "rep").astype(jnp.float32),
        lax.psum(part_sums[5].astype(jnp.bfloat16), "rep").astype(jnp.float32),
        lax.psum(part_sums[6].astype(jnp.bfloat16), "rep").astype(jnp.float32),
        lax.psum(part_sums[7].astype(jnp.bfloat16), "rep").astype(jnp.float32),
        lax.psum(part_sums[8].astype(jnp.bfloat16), "rep").astype(jnp.float32),
        lax.psum(part_sums[9].astype(jnp.bfloat16), "rep").astype(jnp.float32),
        lax.psum(part_sums[10].astype(jnp.bfloat16), "rep").astype(jnp.float32),
    )
    sq_input, sq_attn, sq_feed, live_total = lax.psum(
        (
            jnp.sum(live_mask * stream_in * stream_in),
            jnp.sum(live_mask * attn_out * attn_out),
            jnp.sum(live_mask * feed_out * feed_out),
            jnp.sum(live_mask),
        ),
        ("rep", "shard"),
    )
    denom = live_total * width
    return (
        output,
        input_grad,
        owned[0],
        owned[1],
        owned[2],
        owned[3],
        owned[4],
        owned[5],
        owned[6],
        owned[7],
        owned[8],
        owned[9],
        owned[10],
        jnp.sqrt(sq_input / denom),
        jnp.sqrt(sq_attn / denom),
        jnp.sqrt(sq_feed / denom),
    )


def solution(mesh):
    return jax.shard_map(
        per_device,
        mesh=mesh,
        in_specs=(
            P(("rep", "shard"), None),
            P(("rep", "shard"), None),
            P("rep"),
            P("shard"),
            P("shard", None),
            P("shard", None),
            P("shard", None),
            P("shard", None),
            P("shard", None),
            P("shard", None),
            P("shard"),
            P("shard", None),
            P("shard", None),
            P("shard", None),
        ),
        out_specs=(
            P(("rep", "shard"), None),
            P(("rep", "shard"), None),
            P("shard"),
            P("shard", None),
            P("shard", None),
            P("shard", None),
            P("shard", None),
            P("shard", None),
            P("shard", None),
            P("shard"),
            P("shard", None),
            P("shard", None),
            P("shard", None),
            P(),
            P(),
            P(),
        ),
        check_vma=False,
    )
```

profile of v0, /device:TPU:0, one launch (start us, length us, event | category | flops | bytes accessed | tf_op | source)
XLA Modules:
  0.0 1988.5 jit_solution(15971856994298718647)
XLA Ops:
  10.1 9.5 all-gather.1
  19.6 8.5 all_gather.46
  29.4 40.5 %all-gather.19.cloned.1.call-done = bf16[1536,1536]{1,0:T(8,128)(2,1)} async-done(((bf16[384,1536]{1,0:T(8,128)(2,1)}), bf16[1536,1536]{1,0:T(8,128)(2,1)}) %all-gather.19.cloned.1.call-update) | async-done | bytes 4718608 | tf_op jit(solution)/shard_map/all_gather | solution.py:157
  76.4 117.9 %custom-call.16 = f32[12,1,128,128]{2,3,1,0:T(8,128)S(1)} custom-call(f32[12,1,128,128]{3,2,1,0:T(8,128)S(1)} %add_bitcast_fusion), custom_call_target="InvertDiagBlocksLowerTriangular" | custom-call | tf_op jit(solution)/shard_map/jvp(jit(_solve_triangular))/vmap()/triangular_solve/custom-call.1 | solution.py:89
  216.0 8.1 all-gather.2
  228.1 20.2 %all-gather.15.cloned.1.call-done = bf16[1536,1536]{1,0:T(8,128)(2,1)} async-done(((bf16[384,1536]{1,0:T(8,128)(2,1)}), bf16[1536,1536]{1,0:T(8,128)(2,1)}) %all-gather.15.cloned.1.call-update) | async-done | bytes 4718608 | tf_op jit(solution)/shard_map/all_gather | solution.py:154
  263.0 18.5 all-gather.35.cloned.1.call-done
  285.0 29.7 %all-gather.21.cloned.1.call-done = bf16[512,1536]{0,1:T(8,128)(2,1)} async-done(((bf16[128,1536]{0,1:T(8,128)(2,1)}), bf16[512,1536]{0,1:T(8,128)(2,1)}) %all-gather.21.cloned.1.call-update) | async-done | bytes 1572880 | tf_op jit(solution)/shard_map/all_gather | solution.py:185
  321.8 19.7 while.31
  371.0 36.0 %all-gather.27.cloned.1.call-done = bf16[1536,1536]{1,0:T(8,128)(2,1)} async-done(((bf16[384,1536]{1,0:T(8,128)(2,1)}), bf16[1536,1536]{1,0:T(8,128)(2,1)}) %all-gather.27.cloned.1.call-update) | async-done | bytes 4718608 | tf_op jit(solution)/shard_map/all_gather | solution.py:159
  413.2 118.2 %all-gather.29.cloned.1.call-done = bf16[1536,4096]{1,0:T(8,128)(2,1)} async-done(((bf16[384,4096]{1,0:T(8,128)(2,1)}), bf16[1536,4096]{1,0:T(8,128)(2,1)}) %all-gather.29.cloned.1.call-update) | async-done | bytes 12582928 | tf_op jit(solution)/shard_map/all_gather | solution.py:161
  531.4 7.8 fusion.203
  539.3 116.4 %all-gather.31.cloned.1.call-done = bf16[1536,4096]{1,0:T(8,128)(2,1)} async-done(((bf16[384,4096]{1,0:T(8,128)(2,1)}), bf16[1536,4096]{1,0:T(8,128)(2,1)}) %all-gather.31.cloned.1.call-update) | async-done | bytes 12582928 | tf_op jit(solution)/shard_map/all_gather | solution.py:162
  663.5 116.5 %all-gather.33.cloned.1.call-done = bf16[4096,1536]{1,0:T(8,128)(2,1)} async-done(((bf16[1024,1536]{1,0:T(8,128)(2,1)}), bf16[4096,1536]{1,0:T(8,128)(2,1)}) %all-gather.33.cloned.1.call-update) | async-done | bytes 12582928 | tf_op jit(solution)/shard_map/all_gather | solution.py:163
  780.1 10.2 multiply_convert_fusion
  790.4 10.2 fusion.205
  800.7 9.7 multiply_reduce_fusion
  810.4 8.0 fusion.81
  832.8 8.0 fusion.31
  856.2 8.4 fusion.188
  864.6 41.8 %while.32 = (s32[]{:T(128)}, f32[12,128,128]{2,1,0:T(8,128)}, bf16[4,12,128,128]{3,2,1,0:T(8,128)(2,1)}, f32[4,12,128,128]{3,2,1,0:T(8,128)}, pred[4]{0:T(512)(1...) while((s32[]{:T(128)}, f32[12,128,128]{2,1,0:T(8,128)}, ...), condition=%wide.region_16.19_spmd.clone, body=%wide.region_15.18_spmd.clone.sunk | while | flops 605552640 | bytes 7869556 | solution.py:110
  1022.4 41.7 %reduce-scatter.29.cloned.1.call-done = bf16[384,1536]{1,0:T(8,128)(2,1)} async-done(((bf16[1536,1536]{1,0:T(8,128)(2,1)}), bf16[384,1536]{1,0:T(8,128)(2,1)}) %reduce-scatter.29.cloned.1.call-update) | async-done | bytes 1179664 | tf_op jit(solution)/shard_map/reduce_scatter | solution.py:314
  1064.0 60.5 %reduce-scatter.23.cloned.1.call-done = bf16[384,1536]{1,0:T(8,128)(2,1)} async-done(((bf16[1536,1536]{1,0:T(8,128)(2,1)}), bf16[384,1536]{1,0:T(8,128)(2,1)}) %reduce-scatter.23.cloned.1.call-update) | async-done | bytes 1179664 | tf_op jit(solution)/shard_map/reduce_scatter | solution.py:302
  1124.6 60.6 %reduce-scatter.25.cloned.1.call-done = bf16[384,1536]{1,0:T(8,128)(2,1)} async-done(((bf16[1536,1536]{1,0:T(8,128)(2,1)}), bf16[384,1536]{1,0:T(8,128)(2,1)}) %reduce-scatter.25.cloned.1.call-update) | async-done | bytes 1179664 | tf_op jit(solution)/shard_map/reduce_scatter | solution.py:305
  1185.1 60.1 %reduce-scatter.27.cloned.1.call-done = bf16[384,1536]{1,0:T(8,128)(2,1)} async-done(((bf16[1536,1536]{1,0:T(8,128)(2,1)}), bf16[384,1536]{1,0:T(8,128)(2,1)}) %reduce-scatter.27.cloned.1.call-update) | async-done | bytes 1179664 | tf_op jit(solution)/shard_map/reduce_scatter | solution.py:308
  1245.2 123.7 %reduce-scatter.31.cloned.1.call-done = bf16[384,4096]{1,0:T(8,128)(2,1)} async-done(((bf16[1536,4096]{1,0:T(8,128)(2,1)}), bf16[384,4096]{1,0:T(8,128)(2,1)}) %reduce-scatter.31.cloned.1.call-update) | async-done | bytes 3145744 | tf_op jit(solution)/shard_map/reduce_scatter | solution.py:320
  1368.9 123.9 %reduce-scatter.33.cloned.1.call-done = bf16[384,4096]{1,0:T(8,128)(2,1)} async-done(((bf16[1536,4096]{1,0:T(8,128)(2,1)}), bf16[384,4096]{1,0:T(8,128)(2,1)}) %reduce-scatter.33.cloned.1.call-update) | async-done | bytes 3145744 | tf_op jit(solution)/shard_map/reduce_scatter | solution.py:323
  1492.8 123.9 %reduce-scatter.35.cloned.1.call-done = bf16[1024,1536]{1,0:T(8,128)(2,1)} async-done(((bf16[4096,1536]{1,0:T(8,128)(2,1)}), bf16[1024,1536]{1,0:T(8,128)(2,1)}) %reduce-scatter.35.cloned.1.call-update) | async-done | bytes 3145744 | tf_op jit(solution)/shard_map/reduce_scatter | solution.py:326
  1633.7 40.3 %all-reduce.3 = (f32[]{:T(128)}, f32[]{:T(128)}, f32[]{:T(128)}, f32[]{:T(128)}) all-reduce(f32[]{:T(128)} %get-tuple-element.278, f32[]{:T(128)} %get-tuple-element.326, f32[]{:T(128)} %get-tuple-element.280, f32[]{:T(128)} %get-tuple-element.279), channel_id=1, replica_groups=mesh['rep'=8,'shard'=4] {'rep','shard'}, use_global_device_ids=true, to_apply=%region_52.55 | all-reduce | flops 4 | bytes 32 | tf_op jit(solution)/shard_map/psum | solution.py:343
  1674.0 10.8 all-reduce.6
  1689.7 28.2 %all-reduce.4 = (bf16[384]{0:T(512)(128)(2,1)S(1)}, bf16[384,12]{0,1:T(8,128)(2,1)S(1)}, bf16[384]{0:T(512)(128)(2,1)S(1)}) all-reduce(bf16[384]{0:T(512)(128)(2,1)S(1)} %dynamic-slice.3, bf16[384,12]{0,1:T(8,128)(2,1)S(1)} %copy.335, bf16[384]{0:T(512)(128)(2,1)S(1)} %dynamic-slice.5), channel_id=1, replica_groups=mesh['rep'=8,'shard'=4] {'rep'}, use_global_device_ids=true, to_apply=%region_29.32 | all-reduce | flops 5376 | bytes 21504 | tf_op jit(solution)/shard_map/psum | solution.py:331
  1719.6 238.0 %all-reduce.9.cloned.1.call-done = (bf16[384,1536]{1,0:T(8,128)(2,1)}, bf16[384,1536]{1,0:T(8,128)(2,1)}, bf16[384,1536]{1,0:T(8,128)(2,1)}, bf16[384,1536]{1,0:...) async-done(((bf16[384,1536]{1,0:T(8,128)(2,1)}, bf16[384,1536]{1,0:T(8,128)(2,1)}, ...) | async-done | bytes 15335440 | tf_op jit(solution)/shard_map/psum | solution.py:332
  (545 shorter events, 347.8 us)
Async XLA Ops:
  7.2 62.7 %all-gather.19.cloned.1.call-start = ((), (), s32[]{:S(2)}) async-start(), calls=%async_computation.14 | async-start | bytes 5898240 | tf_op jit(solution)/shard_map/all_gather | solution.py:157
  7.9 191.4 %all-gather.17.cloned.1.call-start = ((), (), s32[]{:S(2)}) async-start(), calls=%async_computation.13 | async-start | bytes 5898240 | tf_op jit(solution)/shard_map/all_gather | solution.py:155
  8.7 198.7 %all-gather.23.cloned.1.call-start = ((), (), s32[]{:S(2)}) async-start(), calls=%async_computation.16 | async-start | bytes 5898240 | tf_op jit(solution)/shard_map/all_gather | solution.py:156
  9.4 238.9 %all-gather.15.cloned.1.call-start = ((), (), s32[]{:S(2)}) async-start(), calls=%async_computation.12 | async-start | bytes 5898240 | tf_op jit(solution)/shard_map/all_gather | solution.py:154
  10.0 271.5 %all-gather.35.cloned.1.call-start = ((), (), s32[]{:S(2)}) async-start(), calls=%async_computation.30 | async-start | bytes 1966080 | tf_op jit(solution)/shard_map/all_gather | solution.py:191
  28.2 46.1 %copy-start.116 = (bf16[1536,12]{0,1:T(8,128)(2,1)}, bf16[1536,12]{0,1:T(8,128)(2,1)S(1)}, u32[]{:S(2)}) copy-start(bf16[1536,12]{0,1:T(8,128)(2,1)S(1)} %all_gather.46) | copy-start | bytes 110596
  29.0 170.4 %copy-start.108 = (f32[128]{0:T(128)}, f32[128]{0:T(128)S(1)}, u32[]{:S(2)}) copy-start(f32[128]{0:T(128)S(1)} %fusion.179) | copy-start | bytes 1540
  74.6 124.3 %copy-start.114 = (f32[128,12]{0,1:T(8,128)}, f32[128,12]{0,1:T(8,128)S(1)}, u32[]{:S(2)}) copy-start(f32[128,12]{0,1:T(8,128)S(1)} %multiply_reduce_fusion.7) | copy-start | bytes 18436
  194.3 60.0 %copy-start = (f32[12,1,128,128]{2,3,1,0:T(8,128)}, f32[12,1,128,128]{2,3,1,0:T(8,128)S(1)}, u32[]{:S(2)}) copy-start(f32[12,1,128,128]{2,3,1,0:T(8,128)S(1)} %custom-call.16) | copy-start | bytes 2359300
  199.0 115.6 %all-gather.21.cloned.1.call-start = ((), (), s32[]{:S(2)}) async-start(), calls=%async_computation.15 | async-start | bytes 1966080 | tf_op jit(solution)/shard_map/all_gather | solution.py:185
  203.2 57.3 %copy-start.16 = (bf16[128,1536]{0,1:T(8,128)(2,1)}, bf16[128,1536]{0,1:T(8,128)(2,1)S(1)}, u32[]{:S(2)}) copy-start(bf16[128,1536]{0,1:T(8,128)(2,1)S(1)} %copy.185) | copy-start | bytes 1179652
  204.9 53.4 %copy-start.9 = (f32[12,128,128]{2,1,0:T(8,128)}, f32[12,128,128]{2,1,0:T(8,128)S(1)}, u32[]{:S(2)}) copy-start(f32[12,128,128]{2,1,0:T(8,128)S(1)} %fusion.105) | copy-start | bytes 2359300
  207.4 143.5 %all-gather.25.cloned.1.call-start = ((), (), s32[]{:S(2)}) async-start(), calls=%async_computation.17 | async-start | bytes 1966080 | tf_op jit(solution)/shard_map/all_gather | solution.py:188
  211.4 195.7 %all-gather.27.cloned.1.call-start = ((), (), s32[]{:S(2)}) async-start(), calls=%async_computation.18 | async-start | bytes 5898240 | tf_op jit(solution)/shard_map/all_gather | solution.py:159
  212.1 319.3 %all-gather.29.cloned.1.call-start = ((), (), s32[]{:S(2)}) async-start(), calls=%async_computation.19 | async-start | bytes 15728640 | tf_op jit(solution)/shard_map/all_gather | solution.py:161
  212.9 442.8 %all-gather.31.cloned.1.call-start = ((), (), s32[]{:S(2)}) async-start(), calls=%async_computation.20 | async-start | bytes 15728640 | tf_op jit(solution)/shard_map/all_gather | solution.py:162
  213.5 566.6 %all-gather.33.cloned.1.call-start = ((), (), s32[]{:S(2)}) async-start(), calls=%async_computation.21 | async-start | bytes 15728640 | tf_op jit(solution)/shard_map/all_gather | solution.py:163
  214.2 724.2 %reduce-scatter.37.cloned.1.call-start = ((), (), s32[]{:S(2)}) async-start(), calls=%async_computation.31 | async-start | bytes 1966080
  843.5 108.3 %reduce-scatter.39.cloned.1.call-start = ((), (), s32[]{:S(2)}) async-start(), calls=%async_computation.32 | async-start | bytes 1966080
  856.0 116.3 %reduce-scatter.43.cloned.1.call-start = ((), (), s32[]{:S(2)}) async-start(), calls=%async_computation.34 | async-start | bytes 1966080
  906.5 115.9 %reduce-scatter.21.cloned.1.call-start = ((), (), s32[]{:S(2)}) async-start(), calls=%async_computation.22 | async-start | bytes 5898240 | tf_op jit(solution)/shard_map/reduce_scatter | solution.py:299
  923.5 140.5 %reduce-scatter.29.cloned.1.call-start = ((), (), s32[]{:S(2)}) async-start(), calls=%async_computation.26 | async-start | bytes 5898240 | tf_op jit(solution)/shard_map/reduce_scatter | solution.py:314
  928.4 196.2 %reduce-scatter.23.cloned.1.call-start = ((), (), s32[]{:S(2)}) async-start(), calls=%async_computation.23 | async-start | bytes 5898240 | tf_op jit(solution)/shard_map/reduce_scatter | solution.py:302
  951.7 233.4 %reduce-scatter.25.cloned.1.call-start = ((), (), s32[]{:S(2)}) async-start(), calls=%async_computation.24 | async-start | bytes 5898240 | tf_op jit(solution)/shard_map/reduce_scatter | solution.py:305
  960.9 284.3 %reduce-scatter.27.cloned.1.call-start = ((), (), s32[]{:S(2)}) async-start(), calls=%async_computation.25 | async-start | bytes 5898240 | tf_op jit(solution)/shard_map/reduce_scatter | solution.py:308
  996.8 372.2 %reduce-scatter.31.cloned.1.call-start = ((), (), s32[]{:S(2)}) async-start(), calls=%async_computation.27 | async-start | bytes 15728640 | tf_op jit(solution)/shard_map/reduce_scatter | solution.py:320
  1004.6 488.2 %reduce-scatter.33.cloned.1.call-start = ((), (), s32[]{:S(2)}) async-start(), calls=%async_computation.28 | async-start | bytes 15728640 | tf_op jit(solution)/shard_map/reduce_scatter | solution.py:323
  1012.2 604.5 %reduce-scatter.35.cloned.1.call-start = ((), (), s32[]{:S(2)}) async-start(), calls=%async_computation.29 | async-start | bytes 15728640 | tf_op jit(solution)/shard_map/reduce_scatter | solution.py:326
  1020.3 668.4 %reduce-scatter.41.cloned.1.call-start = ((), (), s32[]{:S(2)}) async-start(), calls=%async_computation.33 | async-start | bytes 491520
  1022.3 935.4 %all-reduce.9.cloned.1.call-start = ((), (), s32[]{:S(2)}) async-start(), calls=%async_computation.35 | async-start | bytes 30670848 | tf_op jit(solution)/shard_map/psum | solution.py:332
  1630.9 56.8 %copy-start.136 = (f32[128]{0:T(128)S(1)}, f32[128]{0:T(128)}, u32[]{:S(2)}) copy-start(f32[128]{0:T(128)} %copy-done.135) | copy-start | bytes 1540
  1630.9 56.8 %copy-start.23 = (f32[128,1536]{1,0:T(8,128)S(1)}, f32[128,1536]{1,0:T(8,128)}, u32[]{:S(2)}) copy-start(f32[128,1536]{1,0:T(8,128)} %copy-done.22) | copy-start | bytes 2359300
  (137 other events, 730.2 us)
Sparse Core Ops, SparseCore 0:
  9.9 60.0 all-gather.18
  71.8 58.0 all-gather.16
  131.7 57.6 all-gather.22
  191.1 57.1 all-gather.14
  250.5 30.9 all-gather.34
  283.8 30.8 all-gather.20
  317.1 30.9 all-gather.24
  349.9 57.0 all-gather.26
  408.9 122.5 all-gather.28
  533.1 122.5 all-gather.30
  657.5 122.5 all-gather.32
  843.6 30.9 reduce-scatter.36
  878.1 30.9 reduce-scatter.38
  912.5 30.9 reduce-scatter.42
  946.9 57.0 reduce-scatter.20
  1006.9 57.0 reduce-scatter.28
  1067.4 57.0 reduce-scatter.22
  1128.0 57.0 reduce-scatter.24
  1188.1 57.0 reduce-scatter.26
  1248.2 120.7 reduce-scatter.30
  1372.0 120.7 reduce-scatter.32
  1495.9 120.7 reduce-scatter.34
  1620.0 24.5 reduce-scatter.40
  1647.4 310.1 all-reduce.8
where the time goes:
time: 2000 us; the launch traced here: 1990 us
  waiting for transfers between devices  1330 us (66%)
  matrix products  278 us (14%)
  other arithmetic  163 us (8%)
  blocking collectives  105 us (5%)
  local copies, waits for them, and re-layouts  78.5 us (4%)
  between operations  24 us (1%)
    psum x1, waiting for transfers between devices, per_device(): lax.psum(part_sums[1].astype(jnp.bfloat16), 'rep').astype(jnp.float32)  238 us
    reduce_scatter x1, waiting for transfers between devices, per_device(): lax.psum_scatter(g_up.astype(jnp.bfloat16), 'shard', scatter_dimension=0,...  124 us
    reduce_scatter x1, waiting for transfers between devices, per_device(): lax.psum_scatter(g_down.astype(jnp.bfloat16), 'shard', scatter_dimension=...  124 us
    reduce_scatter x1, waiting for transfers between devices, per_device(): lax.psum_scatter(g_gate.astype(jnp.bfloat16), 'shard', scatter_dimension=...  124 us
    all_gather x1, waiting for transfers between devices, per_device(): lax.all_gather(w_gate, 'shard', axis=0, tiled=True)  118 us
    another operation x4, other arithmetic, attend(): jax.scipy.linalg.solve_triangular(system, coupled, lower=True, unit_diago...  118 us
    all_gather x1, waiting for transfers between devices, per_device(): lax.all_gather(w_down, 'shard', axis=0, tiled=True)  117 us
    all_gather x1, waiting for transfers between devices, per_device(): lax.all_gather(w_up, 'shard', axis=0, tiled=True)  116 us
  transfers between devices with their start and end apart: 24, of which 16 were waited for; matrix products, arithmetic and copies ran while one was open for 21% of the time, Pallas kernels for 0%

commit v1 on v0

--- a/solution.py
+++ b/solution.py
@@ -2,9 +2,15 @@
 import jax.numpy as jnp
 from jax import lax
 from jax.sharding import PartitionSpec as P
+from jax.lax import all_gather
 
 eps = 1e-06
 highest = lax.Precision.HIGHEST
+
+
+def manage_the_points(load):
+    v1 = jnp.sum(all_gather(load, "rep"), 0)
+    return v1
 
 
 def rms_norm(value, gain_vec):
@@ -329,7 +335,7 @@
     )
     owned = (
         lax.psum(part_sums[0].astype(jnp.bfloat16), "rep").astype(jnp.float32),
-        lax.psum(part_sums[1].astype(jnp.bfloat16), "rep").astype(jnp.float32),
+        manage_the_points(part_sums[1].astype(jnp.bfloat16)).astype(jnp.float32),
         lax.psum(part_sums[2].astype(jnp.bfloat16), "rep").astype(jnp.float32),
         lax.psum(part_sums[3].astype(jnp.bfloat16), "rep").astype(jnp.float32),
         lax.psum(part_sums[4].astype(jnp.bfloat16), "rep").astype(jnp.float32),

time: 2000 us -> 2060 us (1.030)
  waiting for transfers between devices: 1330 us -> 1390 us
    psum x1, waiting for transfers between devices: 238 us -> 280 us  [per_device(): lax.psum(part_sums[2].astype(jnp.bfloat16), 'rep').astype(jnp.float32)]
  transfers between devices with their start and end apart: 24 -> 25, of which waited for: 16 -> 17; matrix products, arithmetic and copies ran while one was open for 21% -> 21% of each run, Pallas kernels for 0% -> 0%
where the time goes in v1:
time: 2060 us; the launch traced here: 2050 us
  waiting for transfers between devices  1390 us (67%)
  matrix products  278 us (13%)
  other arithmetic  169 us (8%)
  blocking collectives  106 us (5%)
  local copies, waits for them, and re-layouts  79.6 us (4%)
  between operations  23.7 us (1%)
    psum x1, waiting for transfers between devices, per_device(): lax.psum(part_sums[2].astype(jnp.bfloat16), 'rep').astype(jnp.float32)  280 us
    reduce_scatter x1, waiting for transfers between devices, per_device(): lax.psum_scatter(g_up.astype(jnp.bfloat16), 'shard', scatter_dimension=0,...  124 us
    reduce_scatter x1, waiting for transfers between devices, per_device(): lax.psum_scatter(g_down.astype(jnp.bfloat16), 'shard', scatter_dimension=...  124 us
    reduce_scatter x1, waiting for transfers between devices, per_device(): lax.psum_scatter(g_gate.astype(jnp.bfloat16), 'shard', scatter_dimension=...  124 us
    all_gather x1, waiting for transfers between devices, per_device(): lax.all_gather(w_gate, 'shard', axis=0, tiled=True)  118 us
    another operation x4, other arithmetic, attend(): jax.scipy.linalg.solve_triangular(system, coupled, lower=True, unit_diago...  118 us
    all_gather x1, waiting for transfers between devices, per_device(): lax.all_gather(w_down, 'shard', axis=0, tiled=True)  117 us
    all_gather x1, waiting for transfers between devices, per_device(): lax.all_gather(w_up, 'shard', axis=0, tiled=True)  116 us
  transfers between devices with their start and end apart: 25, of which 17 were waited for; matrix products, arithmetic and copies ran while one was open for 21% of the time, Pallas kernels for 0%

profile of v1, /device:TPU:0, one launch (start us, length us, event | category | flops | bytes accessed | tf_op | source)
XLA Modules:
  0.0 2053.6 jit_solution(16950922087343562289)
XLA Ops:
  10.1 9.5 all-gather.2
  19.6 8.5 all_gather.52
  29.3 40.6 %all-gather.21.cloned.1.call-done = bf16[1536,1536]{1,0:T(8,128)(2,1)} async-done(((bf16[384,1536]{1,0:T(8,128)(2,1)}), bf16[1536,1536]{1,0:T(8,128)(2,1)}) %all-gather.21.cloned.1.call-update) | async-done | bytes 4718608 | tf_op jit(solution)/shard_map/all_gather | solution.py:163
  77.1 117.9 %custom-call.16 = f32[12,1,128,128]{2,3,1,0:T(8,128)S(1)} custom-call(f32[12,1,128,128]{3,2,1,0:T(8,128)S(1)} %add_bitcast_fusion), custom_call_target="InvertDiagBlocksLowerTriangular" | custom-call | tf_op jit(solution)/shard_map/jvp(jit(_solve_triangular))/vmap()/triangular_solve/custom-call.1 | solution.py:95
  216.3 8.1 all-gather.3
  228.5 19.0 all-gather.17.cloned.1.call-done
  262.3 18.5 all-gather.37.cloned.1.call-done
  284.2 29.7 %all-gather.23.cloned.1.call-done = bf16[512,1536]{0,1:T(8,128)(2,1)} async-done(((bf16[128,1536]{0,1:T(8,128)(2,1)}), bf16[512,1536]{0,1:T(8,128)(2,1)}) %all-gather.23.cloned.1.call-update) | async-done | bytes 1572880 | tf_op jit(solution)/shard_map/all_gather | solution.py:191
  321.0 19.7 while.31
  370.3 35.9 %all-gather.29.cloned.1.call-done = bf16[1536,1536]{1,0:T(8,128)(2,1)} async-done(((bf16[384,1536]{1,0:T(8,128)(2,1)}), bf16[1536,1536]{1,0:T(8,128)(2,1)}) %all-gather.29.cloned.1.call-update) | async-done | bytes 4718608 | tf_op jit(solution)/shard_map/all_gather | solution.py:165
  412.4 118.2 %all-gather.31.cloned.1.call-done = bf16[1536,4096]{1,0:T(8,128)(2,1)} async-done(((bf16[384,4096]{1,0:T(8,128)(2,1)}), bf16[1536,4096]{1,0:T(8,128)(2,1)}) %all-gather.31.cloned.1.call-update) | async-done | bytes 12582928 | tf_op jit(solution)/shard_map/all_gather | solution.py:167
  538.4 116.4 %all-gather.33.cloned.1.call-done = bf16[1536,4096]{1,0:T(8,128)(2,1)} async-done(((bf16[384,4096]{1,0:T(8,128)(2,1)}), bf16[1536,4096]{1,0:T(8,128)(2,1)}) %all-gather.33.cloned.1.call-update) | async-done | bytes 12582928 | tf_op jit(solution)/shard_map/all_gather | solution.py:168
  662.7 116.5 %all-gather.35.cloned.1.call-done = bf16[4096,1536]{1,0:T(8,128)(2,1)} async-done(((bf16[1024,1536]{1,0:T(8,128)(2,1)}), bf16[4096,1536]{1,0:T(8,128)(2,1)}) %all-gather.35.cloned.1.call-update) | async-done | bytes 12582928 | tf_op jit(solution)/shard_map/all_gather | solution.py:169
  779.2 10.3 multiply_convert_fusion
  789.6 10.2 fusion.205
  799.8 9.7 multiply_reduce_fusion
  809.6 8.1 fusion.81
  832.0 8.0 fusion.31
  855.4 8.3 fusion.188
  863.8 41.9 %while.32 = (s32[]{:T(128)}, f32[12,128,128]{2,1,0:T(8,128)}, bf16[4,12,128,128]{3,2,1,0:T(8,128)(2,1)}, f32[4,12,128,128]{3,2,1,0:T(8,128)}, pred[4]{0:T(512)(1...) while((s32[]{:T(128)}, f32[12,128,128]{2,1,0:T(8,128)}, ...), condition=%wide.region_16.19_spmd.clone, body=%wide.region_15.18_spmd.clone.sunk | while | flops 605552640 | bytes 7869556 | solution.py:116
  1022.7 40.6 %reduce-scatter.29.cloned.1.call-done = bf16[384,1536]{1,0:T(8,128)(2,1)} async-done(((bf16[1536,1536]{1,0:T(8,128)(2,1)}), bf16[384,1536]{1,0:T(8,128)(2,1)}) %reduce-scatter.29.cloned.1.call-update) | async-done | bytes 1179664 | tf_op jit(solution)/shard_map/reduce_scatter | solution.py:320
  1063.3 60.5 %reduce-scatter.23.cloned.1.call-done = bf16[384,1536]{1,0:T(8,128)(2,1)} async-done(((bf16[1536,1536]{1,0:T(8,128)(2,1)}), bf16[384,1536]{1,0:T(8,128)(2,1)}) %reduce-scatter.23.cloned.1.call-update) | async-done | bytes 1179664 | tf_op jit(solution)/shard_map/reduce_scatter | solution.py:308
  1123.8 60.6 %reduce-scatter.25.cloned.1.call-done = bf16[384,1536]{1,0:T(8,128)(2,1)} async-done(((bf16[1536,1536]{1,0:T(8,128)(2,1)}), bf16[384,1536]{1,0:T(8,128)(2,1)}) %reduce-scatter.25.cloned.1.call-update) | async-done | bytes 1179664 | tf_op jit(solution)/shard_map/reduce_scatter | solution.py:311
  1184.4 60.1 %reduce-scatter.27.cloned.1.call-done = bf16[384,1536]{1,0:T(8,128)(2,1)} async-done(((bf16[1536,1536]{1,0:T(8,128)(2,1)}), bf16[384,1536]{1,0:T(8,128)(2,1)}) %reduce-scatter.27.cloned.1.call-update) | async-done | bytes 1179664 | tf_op jit(solution)/shard_map/reduce_scatter | solution.py:314
  1244.5 123.7 %reduce-scatter.31.cloned.1.call-done = bf16[384,4096]{1,0:T(8,128)(2,1)} async-done(((bf16[1536,4096]{1,0:T(8,128)(2,1)}), bf16[384,4096]{1,0:T(8,128)(2,1)}) %reduce-scatter.31.cloned.1.call-update) | async-done | bytes 3145744 | tf_op jit(solution)/shard_map/reduce_scatter | solution.py:326
  1368.2 123.9 %reduce-scatter.33.cloned.1.call-done = bf16[384,4096]{1,0:T(8,128)(2,1)} async-done(((bf16[1536,4096]{1,0:T(8,128)(2,1)}), bf16[384,4096]{1,0:T(8,128)(2,1)}) %reduce-scatter.33.cloned.1.call-update) | async-done | bytes 3145744 | tf_op jit(solution)/shard_map/reduce_scatter | solution.py:329
  1492.1 123.9 %reduce-scatter.35.cloned.1.call-done = bf16[1024,1536]{1,0:T(8,128)(2,1)} async-done(((bf16[4096,1536]{1,0:T(8,128)(2,1)}), bf16[1024,1536]{1,0:T(8,128)(2,1)}) %reduce-scatter.35.cloned.1.call-update) | async-done | bytes 3145744 | tf_op jit(solution)/shard_map/reduce_scatter | solution.py:332
  1632.9 42.2 %all-reduce.3 = (f32[]{:T(128)}, f32[]{:T(128)}, f32[]{:T(128)}, f32[]{:T(128)}) all-reduce(f32[]{:T(128)} %get-tuple-element.278, f32[]{:T(128)} %get-tuple-element.325, f32[]{:T(128)} %get-tuple-element.280, f32[]{:T(128)} %get-tuple-element.279), channel_id=1, replica_groups=mesh['rep'=8,'shard'=4] {'rep','shard'}, use_global_device_ids=true, to_apply=%region_52.55 | all-reduce | flops 4 | bytes 32 | tf_op jit(solution)/shard_map/psum | solution.py:349
  1675.1 10.2 all-reduce.6
  1690.2 27.3 %all-reduce.4 = (bf16[384]{0:T(512)(128)(2,1)S(1)}, bf16[384,12]{0,1:T(8,128)(2,1)S(1)}, bf16[384]{0:T(512)(128)(2,1)S(1)}) all-reduce(bf16[384]{0:T(512)(128)(2,1)S(1)} %dynamic-slice.3, bf16[384,12]{0,1:T(8,128)(2,1)S(1)} %copy.335, bf16[384]{0:T(512)(128)(2,1)S(1)} %dynamic-slice.5), channel_id=1, replica_groups=mesh['rep'=8,'shard'=4] {'rep'}, use_global_device_ids=true, to_apply=%region_29.32 | all-reduce | flops 5376 | bytes 21504 | tf_op jit(solution)/shard_map/psum | solution.py:337
  1719.3 17.6 all-gather.39.cloned.1.call-done
  1744.5 280.3 %all-reduce.9.cloned.1.call-done = (bf16[384,1536]{1,0:T(8,128)(2,1)}, bf16[384,1536]{1,0:T(8,128)(2,1)}, bf16[384,1536]{1,0:T(8,128)(2,1)}, bf16[384,1536]{1,0:...) async-done(((bf16[384,1536]{1,0:T(8,128)(2,1)}, bf16[384,1536]{1,0:T(8,128)(2,1)}, bf16[384,1536]{1,0:T(8,128)(2,1)}, ...) | async-done | bytes 14155792 | tf_op jit(solution)/shard_map/psum | solution.py:339
  (547 shorter events, 363.1 us)
Async XLA Ops:
  7.2 62.7 %all-gather.21.cloned.1.call-start = ((), (), s32[]{:S(2)}) async-start(), calls=%async_computation.14 | async-start | bytes 5898240 | tf_op jit(solution)/shard_map/all_gather | solution.py:163
  7.9 192.2 %all-gather.19.cloned.1.call-start = ((), (), s32[]{:S(2)}) async-start(), calls=%async_computation.13 | async-start | bytes 5898240 | tf_op jit(solution)/shard_map/all_gather | solution.py:161
  8.7 199.0 %all-gather.25.cloned.1.call-start = ((), (), s32[]{:S(2)}) async-start(), calls=%async_computation.16 | async-start | bytes 5898240 | tf_op jit(solution)/shard_map/all_gather | solution.py:162
  9.4 238.0 %all-gather.17.cloned.1.call-start = ((), (), s32[]{:S(2)}) async-start(), calls=%async_computation.12 | async-start | bytes 5898240 | tf_op jit(solution)/shard_map/all_gather | solution.py:160
  10.0 270.7 %all-gather.37.cloned.1.call-start = ((), (), s32[]{:S(2)}) async-start(), calls=%async_computation.30 | async-start | bytes 1966080 | tf_op jit(solution)/shard_map/all_gather | solution.py:197
  28.9 171.2 %copy-start.107 = (f32[128]{0:T(128)}, f32[128]{0:T(128)S(1)}, u32[]{:S(2)}) copy-start(f32[128]{0:T(128)S(1)} %fusion.179) | copy-start | bytes 1540
  29.3 46.8 %copy-start.83 = (pred[128,128]{1,0:T(8,128)(4,1)}, pred[128,128]{1,0:T(8,128)(4,1)S(1)}, u32[]{:S(2)}) copy-start(pred[128,128]{1,0:T(8,128)(4,1)S(1)} %get-tuple-element.355) | copy-start | bytes 49156
  195.0 58.4 %copy-start = (f32[12,1,128,128]{2,3,1,0:T(8,128)}, f32[12,1,128,128]{2,3,1,0:T(8,128)S(1)}, u32[]{:S(2)}) copy-start(f32[12,1,128,128]{2,3,1,0:T(8,128)S(1)} %custom-call.16) | copy-start | bytes 2359300
  199.7 114.1 %all-gather.23.cloned.1.call-start = ((), (), s32[]{:S(2)}) async-start(), calls=%async_computation.15 | async-start | bytes 1966080 | tf_op jit(solution)/shard_map/all_gather | solution.py:191
  203.5 56.2 %copy-start.16 = (bf16[128,1536]{0,1:T(8,128)(2,1)}, bf16[128,1536]{0,1:T(8,128)(2,1)S(1)}, u32[]{:S(2)}) copy-start(bf16[128,1536]{0,1:T(8,128)(2,1)S(1)} %copy.185) | copy-start | bytes 1179652
  205.2 52.3 %copy-start.9 = (f32[12,128,128]{2,1,0:T(8,128)}, f32[12,128,128]{2,1,0:T(8,128)S(1)}, u32[]{:S(2)}) copy-start(f32[12,128,128]{2,1,0:T(8,128)S(1)} %fusion.105) | copy-start | bytes 2359300
  207.7 142.3 %all-gather.27.cloned.1.call-start = ((), (), s32[]{:S(2)}) async-start(), calls=%async_computation.17 | async-start | bytes 1966080 | tf_op jit(solution)/shard_map/all_gather | solution.py:194
  211.7 194.5 %all-gather.29.cloned.1.call-start = ((), (), s32[]{:S(2)}) async-start(), calls=%async_computation.18 | async-start | bytes 5898240 | tf_op jit(solution)/shard_map/all_gather | solution.py:165
  212.4 318.1 %all-gather.31.cloned.1.call-start = ((), (), s32[]{:S(2)}) async-start(), calls=%async_computation.19 | async-start | bytes 15728640 | tf_op jit(solution)/shard_map/all_gather | solution.py:167
  213.2 441.6 %all-gather.33.cloned.1.call-start = ((), (), s32[]{:S(2)}) async-start(), calls=%async_computation.20 | async-start | bytes 15728640 | tf_op jit(solution)/shard_map/all_gather | solution.py:168
  213.8 565.4 %all-gather.35.cloned.1.call-start = ((), (), s32[]{:S(2)}) async-start(), calls=%async_computation.21 | async-start | bytes 15728640 | tf_op jit(solution)/shard_map/all_gather | solution.py:169
  214.5 723.2 %reduce-scatter.37.cloned.1.call-start = ((), (), s32[]{:S(2)}) async-start(), calls=%async_computation.32 | async-start | bytes 1966080
  842.7 108.4 %reduce-scatter.39.cloned.1.call-start = ((), (), s32[]{:S(2)}) async-start(), calls=%async_computation.33 | async-start | bytes 1966080
  855.2 116.5 %reduce-scatter.43.cloned.1.call-start = ((), (), s32[]{:S(2)}) async-start(), calls=%async_computation.35 | async-start | bytes 1966080
  905.7 116.4 %reduce-scatter.21.cloned.1.call-start = ((), (), s32[]{:S(2)}) async-start(), calls=%async_computation.22 | async-start | bytes 5898240 | tf_op jit(solution)/shard_map/reduce_scatter | solution.py:305
  922.7 140.5 %reduce-scatter.29.cloned.1.call-start = ((), (), s32[]{:S(2)}) async-start(), calls=%async_computation.26 | async-start | bytes 5898240 | tf_op jit(solution)/shard_map/reduce_scatter | solution.py:320
  927.7 196.1 %reduce-scatter.23.cloned.1.call-start = ((), (), s32[]{:S(2)}) async-start(), calls=%async_computation.23 | async-start | bytes 5898240 | tf_op jit(solution)/shard_map/reduce_scatter | solution.py:308
  951.1 233.3 %reduce-scatter.25.cloned.1.call-start = ((), (), s32[]{:S(2)}) async-start(), calls=%async_computation.24 | async-start | bytes 5898240 | tf_op jit(solution)/shard_map/reduce_scatter | solution.py:311
  960.3 284.1 %reduce-scatter.27.cloned.1.call-start = ((), (), s32[]{:S(2)}) async-start(), calls=%async_computation.25 | async-start | bytes 5898240 | tf_op jit(solution)/shard_map/reduce_scatter | solution.py:314
  996.2 372.0 %reduce-scatter.31.cloned.1.call-start = ((), (), s32[]{:S(2)}) async-start(), calls=%async_computation.27 | async-start | bytes 15728640 | tf_op jit(solution)/shard_map/reduce_scatter | solution.py:326
  1004.1 488.0 %reduce-scatter.33.cloned.1.call-start = ((), (), s32[]{:S(2)}) async-start(), calls=%async_computation.28 | async-start | bytes 15728640 | tf_op jit(solution)/shard_map/reduce_scatter | solution.py:329
  1011.7 604.2 %reduce-scatter.35.cloned.1.call-start = ((), (), s32[]{:S(2)}) async-start(), calls=%async_computation.29 | async-start | bytes 15728640 | tf_op jit(solution)/shard_map/reduce_scatter | solution.py:332
  1020.1 669.1 %reduce-scatter.41.cloned.1.call-start = ((), (), s32[]{:S(2)}) async-start(), calls=%async_computation.34 | async-start | bytes 491520
  1022.1 714.8 %all-gather.39.cloned.1.call-start = ((), (), s32[]{:S(2)}) async-start(), calls=%async_computation.31 | async-start | bytes 10616832 | tf_op jit(solution)/shard_map/all_gather | solution.py:12
  1022.6 1002.1 %all-reduce.9.cloned.1.call-start = ((), (), s32[]{:S(2)}) async-start(), calls=%async_computation.36 | async-start | bytes 28311552 | tf_op jit(solution)/shard_map/psum | solution.py:339
  1630.2 58.0 %copy-start.135 = (f32[128]{0:T(128)S(1)}, f32[128]{0:T(128)}, u32[]{:S(2)}) copy-start(f32[128]{0:T(128)} %copy-done.134) | copy-start | bytes 1540
  1630.2 58.0 %copy-start.23 = (f32[128,1536]{1,0:T(8,128)S(1)}, f32[128,1536]{1,0:T(8,128)}, u32[]{:S(2)}) copy-start(f32[128,1536]{1,0:T(8,128)} %copy-done.22) | copy-start | bytes 2359300
  (137 other events, 731.7 us)
Sparse Core Ops, SparseCore 0:
  9.9 60.0 all-gather.20
  71.8 57.5 all-gather.18
  131.2 57.3 all-gather.24
  190.3 57.1 all-gather.16
  249.7 30.9 all-gather.36
  283.0 30.8 all-gather.22
  316.2 30.9 all-gather.26
  349.1 57.0 all-gather.28
  408.0 122.5 all-gather.30
  532.3 122.5 all-gather.32
  656.7 122.5 all-gather.34
  842.8 30.9 reduce-scatter.36
  877.4 30.9 reduce-scatter.38
  911.8 30.9 reduce-scatter.42
  946.1 57.0 reduce-scatter.20
  1006.1 57.0 reduce-scatter.28
  1066.7 57.0 reduce-scatter.22
  1127.2 57.0 reduce-scatter.24
  1187.3 57.0 reduce-scatter.26
  1247.4 120.7 reduce-scatter.30
  1371.3 120.7 reduce-scatter.32
  1495.2 120.7 reduce-scatter.34
  1619.3 24.5 reduce-scatter.40
  1645.4 91.4 all-gather.38
  1739.8 284.9 all-reduce.8
